TPU v7x, 32 devices: a whole 2x2x4 slice. The times are simulated.
32 devices in a mesh: row: 8 (over z, y), col: 4 (over x, core).
Axes of the slice: x: 2, y: 2, z: 4, core: 2. Of those that a mesh axis runs over, the one named last changes fastest.
Arguments:
- trail_adjoint: float32 [4096, 4096], P('row', 'col'), may hold values from -6 to 6
- lower_new: float32 [4096, 256], P('row', 'col'), may hold values from -0.09375 to 0.09375
- upper_new: float32 [256, 4096], P('row', 'col'), may hold values from -0.09375 to 0.09375
- lower_old_top: float32 [256, 256], replicated, may hold values from -0.375 to 0.375
- lower_old: float32 [4096, 256], P('row', 'col'), may hold values from -0.09375 to 0.09375
- upper_old_left: float32 [256, 256], replicated, may hold values from -0.375 to 0.375
- upper_old: float32 [256, 4096], P('row', 'col'), may hold values from -0.09375 to 0.09375
- diag_lower_new: float32 [256, 256], replicated, as said below
- diag_upper_new: float32 [256, 256], replicated, as said below
- inverse_lower_new: float32 [256, 256], replicated, as said below
- inverse_upper_new: float32 [256, 256], replicated, as said below
- diag_lower_old: float32 [256, 256], replicated, as said below
- diag_upper_old: float32 [256, 256], replicated, as said below
- inverse_lower_old: float32 [256, 256], replicated, as said below
- inverse_upper_old: float32 [256, 256], replicated, as said below
Outputs:
- corner_old: float32 [256, 256], replicated
- strip_top: float32 [256, 256], replicated
- strip_bottom: float32 [4096, 256], P(('row', 'col'))
- band_left: float32 [256, 256], replicated
- band_right: float32 [256, 4096], P(None, 'col')
Inputs may be any that keep to these rules, and one draw needn't show every extreme that they name: `diag_lower_new`: unit lower triangular. `diag_upper_new`: upper triangular, diagonal from 1 to 2. `inverse_lower_new`: the inverse of diag_lower_new. `inverse_upper_new`: the inverse of diag_upper_new. `diag_lower_old`: unit lower triangular. `diag_upper_old`: upper triangular, diagonal from 1 to 2. `inverse_lower_old`: the inverse of diag_lower_old. `inverse_upper_old`: the inverse of diag_upper_old.
All inputs are finite; a program needn't handle non-finite values.
Results may differ from a plain program's by a relative error of at most 0.000075.
Values sent between devices are 32-bit elements; how exact they have to be, the bound alone decides.
A program may use at most 128 MiB of HBM per device.

v0:
```python
import jax
import jax.numpy as jnp
from jax import lax
from jax.sharding import PartitionSpec as P

precise = lax.Precision.HIGHEST


def times_trans(left, right):
    return lax.dot_general(left, right, (((1,), (1,)), ((), ())), precision=precise)


def trans_times(left, right):
    return lax.dot_general(left, right, (((0,), (0,)), ((), ())), precision=precise)


def diag_adjoint(lower_factor, upper_factor, lower_inverse, upper_inverse, lower_grad, upper_grad):
    inner = jnp.tril(trans_times(lower_factor, lower_grad), -1) + jnp.triu(
        times_trans(upper_grad, upper_factor)
    )
    return times_trans(trans_times(lower_inverse, inner), upper_inverse)


def upper_inner(terms):
    summed = lax.psum(terms, "col")
    return summed


def lower_inner(terms):
    summed = lax.psum(terms, "row")
    return summed


def body(
    trail_adjoint,
    lower_new,
    upper_new,
    lower_old_top,
    lower_old,
    upper_old_left,
    upper_old,
    diag_lower_new,
    diag_upper_new,
    inverse_lower_new,
    inverse_upper_new,
    diag_lower_old,
    diag_upper_old,
    inverse_lower_old,
    inverse_upper_old,
):
    width = inverse_lower_new.shape[0]
    lower_full_new, lower_full_old = (
        lax.all_gather(lower_new, "col", axis=1, tiled=True),
        lax.all_gather(lower_old, "col", axis=1, tiled=True),
    )
    upper_full_new, upper_full_old = (
        lax.all_gather(upper_new, "row", axis=0, tiled=True),
        lax.all_gather(upper_old, "row", axis=0, tiled=True),
    )
    lower_stack = jnp.concatenate((lower_full_new, lower_full_old), axis=1)
    upper_stack = jnp.concatenate((upper_full_new, upper_full_old), axis=0)
    portion = trail_adjoint.shape[0] // lax.axis_size("col")
    offset = lax.axis_index("col") * portion
    lower_adj = lax.psum(-times_trans(trail_adjoint, upper_stack), "col")
    lower_adj_new = lower_adj[:, :width]
    lower_adj_old = lower_adj[:, width:]
    strip_new = times_trans(lower_adj_new, inverse_upper_new)
    upper_adj = lax.psum(-trans_times(lower_stack, trail_adjoint), "row")
    band_new = trans_times(inverse_lower_new, upper_adj[:width])
    outer_new = upper_inner(
        (times_trans(band_new, upper_full_new), times_trans(band_new, upper_full_old))
    )
    inner_new = lower_inner(
        (trans_times(lower_full_new, strip_new), trans_times(lower_full_old, strip_new))
    )
    corner_new = diag_adjoint(
        diag_lower_new,
        diag_upper_new,
        inverse_lower_new,
        inverse_upper_new,
        -outer_new[0],
        -inner_new[0],
    )
    strip_top = times_trans(
        -(times_trans(corner_new, upper_old_left) + outer_new[1]), inverse_upper_old
    )
    strip_bottom = times_trans(
        lower_adj_old - times_trans(strip_new, upper_old_left), inverse_upper_old
    )
    band_left = trans_times(
        inverse_lower_old, -(trans_times(lower_old_top, corner_new) + inner_new[1])
    )
    band_right = trans_times(
        inverse_lower_old, upper_adj[width:] - trans_times(lower_old_top, band_new)
    )
    outer_old = upper_inner(times_trans(band_right, upper_full_old))
    inner_old = lower_inner(trans_times(lower_full_old, strip_bottom))
    lower_grad = -(times_trans(band_left, upper_old_left) + outer_old)
    upper_grad = -(trans_times(lower_old_top, strip_top) + inner_old)
    corner_old = diag_adjoint(
        diag_lower_old, diag_upper_old, inverse_lower_old, inverse_upper_old, lower_grad, upper_grad
    )
    strip_bottom = lax.dynamic_slice_in_dim(strip_bottom, offset, portion, 0)
    return (corner_old, strip_top, strip_bottom, band_left, band_right)


def solution(mesh):
    return jax.shard_map(
        body,
        mesh=mesh,
        in_specs=(
            P("row", "col"),
            P("row", "col"),
            P("row", "col"),
            P(),
            P("row", "col"),
            P(),
            P("row", "col"),
            P(),
            P(),
            P(),
            P(),
            P(),
            P(),
            P(),
            P(),
        ),
        out_specs=(P(), P(), P(("row", "col"), None), P(), P(None, "col")),
        check_vma=False,
    )
```

profile of v0, /device:TPU:0, one launch (start us, length us, event | category | flops | bytes accessed | tf_op | source)
XLA Modules:
  0.0 336.3 jit_solution(6877117094611444565)
XLA Ops:
  7.2 0.7 all-gather.3.cloned.1.call-update
  8.0 0.7 all-gather.5.cloned.1.call-update
  8.7 8.9 %all_gather.13 = f32[512,256]{0,1:T(8,128)S(1)} all-gather(f32[512,64]{0,1:T(8,128)} %param.19), channel_id=1, replica_groups=mesh['row'=8,'col'=4] {'col'}, dimensions={1}, use_global_device_ids=true | all-gather | bytes 655360 | tf_op jit(solution)/shard_map/all_gather | solution.py:54
  17.6 35.6 %all-gather.3.cloned.1.call-done = f32[256,1024]{1,0:T(8,128)} async-done(((f32[32,1024]{1,0:T(8,128)}), f32[256,1024]{1,0:T(8,128)}) %all-gather.3.cloned.1.call-update) | async-done | bytes 1048592 | tf_op jit(solution)/shard_map/all_gather | solution.py:57
  53.1 41.1 %all-gather.5.cloned.1.call-done = f32[256,1024]{1,0:T(8,128)} async-done(((f32[32,1024]{1,0:T(8,128)}), f32[256,1024]{1,0:T(8,128)}) %all-gather.5.cloned.1.call-update) | async-done | bytes 1048592 | tf_op jit(solution)/shard_map/all_gather | solution.py:58
  94.3 6.0 %fusion.7 = f32[512,512]{0,1:T(8,128)} fusion(f32[512,1024]{1,0:T(8,128)S(1)} %copy-done, f32[256,1024]{1,0:T(8,128)} %all-gather.5.cloned.1.call-done, f32[256,1024]{1,0:T(8,128)} %all-gather.3.cloned.1.call-done), kind=kOutput, calls=%fused_computation.6 | convolution fusion | flops 3222011904 | bytes 5242880 | tf_op jit(solution)/shard_map/dot_general | solution.py:10
  100.4 7.8 %all_gather.12 = f32[512,256]{0,1:T(8,128)S(1)} all-gather(f32[512,64]{0,1:T(8,128)S(1)} %copy-done.22), channel_id=1, replica_groups=mesh['row'=8,'col'=4] {'col'}, dimensions={1}, use_global_device_ids=true | all-gather | bytes 655360 | tf_op jit(solution)/shard_map/all_gather | solution.py:53
  108.2 4.9 %convolution_negate_fusion = f32[512,1024]{1,0:T(8,128)} fusion(f32[512,1024]{1,0:T(8,128)S(1)} %copy-done, f32[512,256]{0,1:T(8,128)S(1)} %all_gather.13, f32[512,256]{0,1:T(8,128)S(1)} %all_gather.12), kind=kOutput, calls=%fused_computation.4 | convolution fusion | flops 3222011904 | bytes 5242880 | tf_op jit(solution)/shard_map/dot_general | solution.py:14
  113.2 22.4 %all-reduce.6.cloned.1.call-done = f32[512,512]{0,1:T(8,128)} async-done(((f32[512,512]{0,1:T(8,128)}), f32[512,512]{0,1:T(8,128)}) %all-reduce.6.cloned.1.call-update) | async-done | bytes 1048592 | tf_op jit(solution)/shard_map/psum | solution.py:64
  135.5 2.2 fusion.26
  137.7 1.7 convolution_bitcast_fusion.4
  139.5 1.7 convolution_bitcast_fusion.6
  141.2 0.7 convolution_subtract_fusion
  141.9 1.0 fusion.40
  142.9 0.8 copy-done.3
  143.7 1.7 convolution_bitcast_fusion.1
  145.7 123.1 %all-reduce.8.cloned.1.call-done = (f32[512,1024]{1,0:T(8,128)}, f32[256,256]{0,1:T(8,128)}, f32[256,256]{0,1:T(8,128)}, f32[256,256]{0,1:T(8,128)}) async-done(((f32[512,1024]{1,0:T(8,128)}, f32[256,256]{0,1:T(8,128)}, f32[256,256]{0,1:T(8,128)}, f32[256,256]{0,1:T(8,128)}), (f32[512,1024]{1,0:T(8,128)}, f32[256,256]{0,1:T(8,128)}, f32[256,256]{0,1:T(8,128)}, ...) | async-done | bytes 2883600 | tf_op jit(solution)/shard_map/psum | solution.py:68
  268.8 3.2 fusion.21
  272.0 1.1 fusion.10
  273.2 1.8 fusion.36
  275.0 2.5 fusion.32
  277.5 2.5 fusion.38
  280.0 2.5 fusion.37
  282.6 1.6 constant_dynamic-slice_fusion
  284.2 1.3 copy.21
  285.5 31.3 %all-reduce.10.cloned.1.call-done = (f32[256,256]{1,0:T(8,128)}, f32[256,256]{1,0:T(8,128)}, f32[256,256]{1,0:T(8,128)}) async-done(((f32[256,256]{1,0:T(8,128)}, f32[256,256]{1,0:T(8,128)}, f32[256,256]{1,0:T(8,128)}), (f32[256,256]{1,0:T(8,128)}, f32[256,256]{1,0:T(8,128)}, f32[256,256]{1,0:T(8,128)})) %all-reduce.10.cloned.1.call-update) | async-done | bytes 786448 | tf_op jit(solution)/shard_map/psum | solution.py:25
  316.8 1.7 fusion.20
  318.5 1.6 fusion.19
  320.2 1.8 fusion.33
  326.4 0.6 fusion.11
  327.6 1.3 fusion.42
  328.9 0.8 copy.20
  (63 shorter events, 5.4 us)
Async XLA Ops:
  7.2 87.1 %copy-start = (f32[512,1024]{1,0:T(8,128)S(1)}, f32[512,1024]{1,0:T(8,128)}, u32[]{:S(2)}) copy-start(f32[512,1024]{1,0:T(8,128)} %param.15) | copy-start | bytes 6291460
  7.2 46.0 %all-gather.3.cloned.1.call-start = ((), (), s32[]{:S(2)}) async-start(), calls=%async_computation | async-start | bytes 1179648 | tf_op jit(solution)/shard_map/all_gather | solution.py:57
  7.9 86.4 %all-gather.5.cloned.1.call-start = ((), (), s32[]{:S(2)}) async-start(), calls=%async_computation.1 | async-start | bytes 1179648 | tf_op jit(solution)/shard_map/all_gather | solution.py:58
  8.7 126.9 %all-reduce.6.cloned.1.call-start = ((), (), s32[]{:S(2)}) async-start(), calls=%async_computation.2 | async-start | bytes 2097152 | tf_op jit(solution)/shard_map/psum | solution.py:64
  17.6 82.8 %copy-start.22 = (f32[512,64]{0,1:T(8,128)S(1)}, f32[512,64]{0,1:T(8,128)}, u32[]{:S(2)}) copy-start(f32[512,64]{0,1:T(8,128)} %param.16) | copy-start | bytes 393220
  100.4 168.4 %all-reduce.8.cloned.1.call-start = ((), (), s32[]{:S(2)}) async-start(), calls=%async_computation.3 | async-start | bytes 5767168 | tf_op jit(solution)/shard_map/psum | solution.py:68
  113.2 28.0 %copy-start.7 = (f32[256,256]{1,0:T(8,128)S(1)}, f32[256,256]{1,0:T(8,128)}, u32[]{:S(2)}) copy-start(f32[256,256]{1,0:T(8,128)} %param.20) | copy-start | bytes 786436
  135.5 5.7 %copy-start.14 = (f32[512,512]{0,1:T(8,128)S(1)}, f32[512,512]{0,1:T(8,128)}, u32[]{:S(2)}) copy-start(f32[512,512]{0,1:T(8,128)} %all-reduce.6.cloned.1.call-done) | copy-start | bytes 3145732
  137.7 4.2 %copy-start.5 = (f32[256,256]{1,0:T(8,128)S(1)}, f32[256,256]{1,0:T(8,128)}, u32[]{:S(2)}) copy-start(f32[256,256]{1,0:T(8,128)} %param.29) | copy-start | bytes 786436
  142.9 0.8 copy-start.3
  143.7 125.1 %copy-start.12 = (f32[256,256]{1,0:T(8,128)S(1)}, f32[256,256]{1,0:T(8,128)}, u32[]{:S(2)}) copy-start(f32[256,256]{1,0:T(8,128)} %param.24) | copy-start | bytes 786436
  145.4 126.6 %copy-start.9 = (f32[256,256]{1,0:T(8,128)S(1)}, f32[256,256]{1,0:T(8,128)}, u32[]{:S(2)}) copy-start(f32[256,256]{1,0:T(8,128)} %param.18) | copy-start | bytes 786436
  145.4 171.4 %all-reduce.10.cloned.1.call-start = ((), (), s32[]{:S(2)}) async-start(), calls=%async_computation.4 | async-start | bytes 1572864 | tf_op jit(solution)/shard_map/psum | solution.py:25
  268.8 3.2 copy-start.11
  272.0 1.1 copy-start.4
  272.0 3.0 copy-start.2
  273.2 4.4 %copy-start.1 = (f32[256,1024]{1,0:T(8,128)S(1)}, f32[256,1024]{1,0:T(8,128)}, u32[]{:S(2)}) copy-start(f32[256,1024]{1,0:T(8,128)} %all-gather.5.cloned.1.call-done) | copy-start | bytes 3145732
  285.5 36.5 %copy-start.13 = (f32[256,256]{1,0:T(8,128)S(1)}, f32[256,256]{1,0:T(8,128)}, u32[]{:S(2)}) copy-start(f32[256,256]{1,0:T(8,128)} %param.25) | copy-start | bytes 786436
  285.5 37.1 %copy-start.8 = (f32[256,256]{1,0:T(8,128)S(1)}, f32[256,256]{1,0:T(8,128)}, u32[]{:S(2)}) copy-start(f32[256,256]{1,0:T(8,128)} %param.20) | copy-start | bytes 786436
  316.8 5.8 %copy-start.21 = (f32[256,256]{1,0:T(8,128)S(1)}, f32[256,256]{1,0:T(8,128)}, u32[]{:S(2)}) copy-start(f32[256,256]{1,0:T(8,128)} %get-tuple-element.16) | copy-start | bytes 786436
  316.8 6.3 %copy-start.10 = (f32[256,256]{1,0:T(8,128)S(1)}, f32[256,256]{1,0:T(8,128)}, u32[]{:S(2)}) copy-start(f32[256,256]{1,0:T(8,128)} %param.18) | copy-start | bytes 786436
  316.8 6.3 %copy-start.19 = (f32[256,256]{0,1:T(8,128)S(1)}, f32[256,256]{0,1:T(8,128)}, u32[]{:S(2)}) copy-start(f32[256,256]{0,1:T(8,128)} %get-tuple-element.11) | copy-start | bytes 786436
  320.1 4.0 %copy-start.6 = (f32[256,256]{1,0:T(8,128)S(1)}, f32[256,256]{1,0:T(8,128)}, u32[]{:S(2)}) copy-start(f32[256,256]{1,0:T(8,128)} %param.29) | copy-start | bytes 786436
  322.0 2.5 copy-start.18
  323.1 2.1 copy-start.20
  323.7 2.1 copy-start.17
  323.7 2.7 copy-start.16
  324.6 3.1 copy-start.15
Sparse Core Ops, SparseCore 0:
  10.1 42.9 all-gather.2
  55.3 38.9 all-gather.4
  100.5 34.9 all-reduce.5
  145.6 123.1 all-reduce.7
  282.7 34.0 all-reduce.9
where the time goes:
time: 337 us; the launch traced here: 336 us
  waiting for transfers between devices  255 us (76%)
  matrix products  45.5 us (14%)
  blocking collectives  16.7 us (5%)
  between operations  14.2 us (4%)
  local copies, waits for them, and re-layouts  4.61 us (1%)
    psum x1, waiting for transfers between devices, body(): upper_adj = lax.psum(-trans_times(lower_stack, trail_adjoint), 'row')  123 us
    all_gather x1, waiting for transfers between devices, body(): lax.all_gather(upper_old, 'row', axis=0, tiled=True)  41.1 us
    all_gather x1, waiting for transfers between devices, body(): lax.all_gather(upper_new, 'row', axis=0, tiled=True)  35.6 us
    psum x1, waiting for transfers between devices, upper_inner(): summed = lax.psum(terms, 'col')  31.3 us
    dot_general x14, matrix products, times_trans(): lax.dot_general(left, right, (((1,), (1,)), ((), ())), precision=precise)  23 us
    dot_general x14, matrix products, trans_times(): lax.dot_general(left, right, (((0,), (0,)), ((), ())), precision=precise)  22.5 us
    psum x1, waiting for transfers between devices, body(): lower_adj = lax.psum(-times_trans(trail_adjoint, upper_stack), 'col')  22.4 us
    all_gather x1, blocking collectives, body(): lax.all_gather(lower_old, 'col', axis=1, tiled=True)  8.86 us
  transfers between devices with their start and end apart: 5, of which 5 were waited for; matrix products, arithmetic and copies ran while one was open for 2% of the time, Pallas kernels for 0%

commit v1 on v0

v1 whole, which is shorter than its diff:
```python
import jax
import jax.numpy as jnp
from jax import lax
from jax.sharding import PartitionSpec as P

precise = lax.Precision.HIGH


def dot(left, right, a, b):
    return lax.dot_general(left, right, (((a,), (b,)), ((), ())), precision=precise)


def body(an, ln, un, lot, lo, uol, uo, dln, dun, iln, iun, dlo, duo, ilo, iuo):
    width = iln.shape[0]
    uppers = lax.all_gather(jnp.concatenate((un[None], uo[None])), "row", axis=1, tiled=True)
    lowers = lax.all_gather(jnp.concatenate((ln[None], lo[None])), "col", axis=2, tiled=True)
    un, uo = uppers[0], uppers[1]
    ln, lo = lowers[0], lowers[1]
    mix_u = dot(dot(iuo, uol, 1, 0), iun, 1, 0)
    mix_l = dot(dot(iln, lot, 1, 0), ilo, 1, 0)
    ut = dot(iuo, uo, 1, 0) - dot(mix_u, un, 1, 0)
    lt = dot(lo, ilo, 1, 0) - dot(ln, mix_l, 1, 0)
    strip = -dot(an, ut, 1, 1)
    band = -dot(lt, an, 0, 0)
    left = -dot(band, un, 1, 1)
    both = -dot(jnp.concatenate((ln, lt), axis=1), strip, 0, 0)
    small = lax.psum(jnp.concatenate((left, both), axis=0), ("row", "col"))
    strip = lax.psum_scatter(strip, "col", scatter_dimension=0, tiled=True)
    band = lax.psum(band, "row")
    band_left = dot(small[:width], iun, 1, 1)
    strip_top = dot(iln, small[width : 2 * width], 0, 0)
    corner = small[2 * width :]
    return (corner, strip_top, strip, band_left, band)


def solution(mesh):
    split, whole = P("row", "col"), P()
    return jax.shard_map(
        body,
        mesh=mesh,
        in_specs=(split, split, split, whole, split, whole, split) + (whole,) * 8,
        out_specs=(P(), P(), P(("row", "col"), None), P(), P(None, "col")),
        check_vma=False,
    )
```

time: 337 us -> 332 us (0.985)
  waiting for transfers between devices: 255 us -> 288 us
  matrix products: 45.5 us -> 15.8 us
  blocking collectives: 16.7 us -> 0 us
  local copies, waits for them, and re-layouts: 4.61 us -> 9.28 us
  other arithmetic: 0.01 us -> 4.48 us
    psum x3 -> x2, waiting for transfers between devices: 177 us -> 208 us  [the longest x1 127 us: body(): small = lax.psum(jnp.concatenate((left, both), axis=0), ('row', 'col'))]
    dot_general x28 -> x14, matrix products: 45.5 us -> 15.8 us  [dot(): lax.dot_general(left, right, (((a,), (b,)), ((), ())), precision=precise)]
    reduce_scatter x0 -> x1, waiting for transfers between devices: none -> 17.2 us  [body(): strip = lax.psum_scatter(strip, 'col', scatter_dimension=0, tiled=True)]
    all_gather x2 -> x0, blocking collectives: 16.7 us -> none  [the longest x1 8.86 us: body(): lax.all_gather(lower_old, 'col', axis=1, tiled=True)]
    all_gather x2, waiting for transfers between devices: 76.7 us -> 61.9 us  [the longest x1 46.1 us: body(): lax.all_gather(jnp.concatenate((un[None], uo[None])), 'row', axis=1, tile...]
    concatenate x0 -> x3, other arithmetic: none -> 4.48 us  [the longest x1 1.84 us: body(): jnp.concatenate((ln[None], lo[None]))]
  transfers between devices with their start and end apart: 5 -> 5, of which waited for: 5 -> 5; matrix products, arithmetic and copies ran while one was open for 2% -> 5% of each run, Pallas kernels for 0% -> 0%
where the time goes in v1:
time: 332 us
  waiting for transfers between devices  288 us (87%)
  matrix products  15.8 us (5%)
  between operations  14 us (4%)
  local copies, waits for them, and re-layouts  9.28 us (3%)
  other arithmetic  4.48 us (1%)
    psum x1, waiting for transfers between devices, body(): small = lax.psum(jnp.concatenate((left, both), axis=0), ('row', 'col'))  127 us
    psum x1, waiting for transfers between devices, body(): band = lax.psum(band, 'row')  80.5 us
    all_gather x1, waiting for transfers between devices, body(): lax.all_gather(jnp.concatenate((un[None], uo[None])), 'row', axis=1, tile...  46.1 us
    reduce_scatter x1, waiting for transfers between devices, body(): strip = lax.psum_scatter(strip, 'col', scatter_dimension=0, tiled=True)  17.2 us
    dot_general x14, matrix products, dot(): lax.dot_general(left, right, (((a,), (b,)), ((), ())), precision=precise)  15.8 us
    all_gather x1, waiting for transfers between devices, body(): lax.all_gather(jnp.concatenate((ln[None], lo[None])), 'col', axis=2, tile...  15.8 us
  transfers between devices with their start and end apart: 5, of which 5 were waited for; matrix products, arithmetic and copies ran while one was open for 5% of the time, Pallas kernels for 0%

profile of v1, /device:TPU:0, one launch (start us, length us, event | category | flops | bytes accessed | tf_op | source)
XLA Modules:
  0.0 331.9 jit_solution(3750939363003081247)
XLA Ops:
  7.3 1.8 pad_maximum_fusion.1
  9.1 0.0 all-gather.5.cloned.1.call-start
  9.2 1.7 pad_maximum_fusion.2
  10.9 0.0 all-reduce.3.cloned.1.call-start
  10.9 1.3 fusion.10
  12.3 0.3 fusion.11
  12.6 0.3 fusion.12
  12.9 1.0 fusion.13
  13.8 15.8 %all-gather.3.cloned.1.call-done = f32[2,512,256]{1,2,0:T(8,128)} async-done(((f32[2,512,64]{1,2,0:T(8,128)}), f32[2,512,256]{1,2,0:T(8,128)}) %all-gather.3.cloned.1.call-update) | async-done | bytes 1048592 | tf_op jit(solution)/shard_map/all_gather | solution.py:16
  29.6 2.0 slice_bitcast_fusion.5
  31.6 1.5 fusion.5
  33.1 0.5 convolution_subtract_fusion
  33.5 0.8 copy-done.2
  34.3 1.1 convolution_negate_fusion
  35.4 46.1 %all-gather.5.cloned.1.call-done = f32[2,256,1024]{2,1,0:T(8,128)} async-done(((f32[2,32,1024]{2,1,0:T(8,128)}), f32[2,256,1024]{2,1,0:T(8,128)}) %all-gather.5.cloned.1.call-update) | async-done | bytes 2097168 | tf_op jit(solution)/shard_map/all_gather | solution.py:15
  81.5 2.5 fusion.4
  84.0 1.0 fusion
  85.0 1.9 convolution_negate_fusion.2
  87.0 0.6 convolution_negate_fusion.1
  87.6 0.7 convolution_negate_fusion.3
  88.3 0.9 pad_maximum_fusion
  89.3 0.5 reduce-scatter.2.cloned.1.call-update
  89.9 0.5 all-reduce.5.cloned.1.call-update
  90.5 127.4 %all-reduce.3.cloned.1.call-done = f32[768,256]{1,0:T(8,128)} async-done(((f32[768,256]{1,0:T(8,128)}), f32[768,256]{1,0:T(8,128)}) %all-reduce.3.cloned.1.call-update) | async-done | bytes 786448 | tf_op jit(solution)/shard_map/psum | solution.py:27
  217.9 1.3 convolution_bitcast_fusion.1
  219.2 0.8 copy.16
  220.1 1.7 slice.32
  221.7 2.0 fusion.6
  223.7 17.2 %reduce-scatter.2.cloned.1.call-done = f32[128,256]{0,1:T(8,128)} async-done(((f32[512,256]{0,1:T(8,128)}), f32[128,256]{0,1:T(8,128)}) %reduce-scatter.2.cloned.1.call-update) | async-done | bytes 131088 | tf_op jit(solution)/shard_map/reduce_scatter | solution.py:28
  240.9 1.7 copy.17
  242.6 80.5 %all-reduce.5.cloned.1.call-done = f32[256,1024]{1,0:T(8,128)} async-done(((f32[256,1024]{1,0:T(8,128)}), f32[256,1024]{1,0:T(8,128)}) %all-reduce.5.cloned.1.call-update) | async-done | bytes 1048592 | tf_op jit(solution)/shard_map/psum | solution.py:29
  323.1 2.3 copy.20
  (33 shorter events, 0.2 us)
Async XLA Ops:
  7.2 27.2 %copy-start = (f32[512,1024]{1,0:T(8,128)S(1)}, f32[512,1024]{1,0:T(8,128)}, u32[]{:S(2)}) copy-start(f32[512,1024]{1,0:T(8,128)} %param.15) | copy-start | bytes 6291460
  7.2 5.1 %copy-start.8 = (f32[256,256]{1,0:T(8,128)S(1)}, f32[256,256]{1,0:T(8,128)}, u32[]{:S(2)}) copy-start(f32[256,256]{1,0:T(8,128)} %param.24) | copy-start | bytes 786436
  7.2 5.4 %copy-start.11 = (f32[256,256]{1,0:T(8,128)S(1)}, f32[256,256]{1,0:T(8,128)}, u32[]{:S(2)}) copy-start(f32[256,256]{1,0:T(8,128)} %param.25) | copy-start | bytes 786436
  7.2 5.4 %copy-start.13 = (f32[256,256]{1,0:T(8,128)S(1)}, f32[256,256]{1,0:T(8,128)}, u32[]{:S(2)}) copy-start(f32[256,256]{1,0:T(8,128)} %param.20) | copy-start | bytes 786436
  7.2 5.6 %copy-start.10 = (f32[256,256]{1,0:T(8,128)S(1)}, f32[256,256]{1,0:T(8,128)}, u32[]{:S(2)}) copy-start(f32[256,256]{1,0:T(8,128)} %param.23) | copy-start | bytes 786436
  7.2 22.4 %all-gather.3.cloned.1.call-start = ((), (), s32[]{:S(2)}) async-start(), calls=%async_computation.1 | async-start | bytes 1310720 | tf_op jit(solution)/shard_map/all_gather | solution.py:16
  9.1 72.4 %all-gather.5.cloned.1.call-start = ((), (), s32[]{:S(2)}) async-start(), calls=%async_computation.2 | async-start | bytes 2359296 | tf_op jit(solution)/shard_map/all_gather | solution.py:15
  10.9 207.0 %all-reduce.3.cloned.1.call-start = ((), (), s32[]{:S(2)}) async-start(), calls=%async_computation.3 | async-start | bytes 1572864 | tf_op jit(solution)/shard_map/psum | solution.py:27
  29.6 3.4 %copy-start.6 = (f32[2,512,256]{1,2,0:T(8,128)S(1)}, f32[2,512,256]{1,2,0:T(8,128)}, u32[]{:S(2)}) copy-start(f32[2,512,256]{1,2,0:T(8,128)} %all-gather.3.cloned.1.call-done) | copy-start | bytes 3145732
  33.5 0.8 copy-start.2
  35.4 52.2 %copy-start.1 = (f32[256,1024]{1,0:T(8,128)}, f32[256,1024]{1,0:T(8,128)S(1)}, u32[]{:S(2)}) copy-start(f32[256,1024]{1,0:T(8,128)S(1)} %convolution_negate_fusion) | copy-start | bytes 3145732
  81.5 2.5 copy-start.4
  81.5 2.5 copy-start.12
  85.0 2.0 copy-start.3
  85.0 2.0 copy-start.7
  87.0 1.3 copy-start.5
  88.3 129.6 %copy-start.9 = (f32[256,256]{1,0:T(8,128)S(1)}, f32[256,256]{1,0:T(8,128)}, u32[]{:S(2)}) copy-start(f32[256,256]{1,0:T(8,128)} %param.22) | copy-start | bytes 786436
  89.3 151.6 %reduce-scatter.2.cloned.1.call-start = ((), (), s32[]{:S(2)}) async-start(), calls=%async_computation.4 | async-start | bytes 655360 | tf_op jit(solution)/shard_map/reduce_scatter | solution.py:28
  89.9 233.2 %all-reduce.5.cloned.1.call-start = ((), (), s32[]{:S(2)}) async-start(), calls=%async_computation.5 | async-start | bytes 2097152 | tf_op jit(solution)/shard_map/psum | solution.py:29
Sparse Core Ops, SparseCore 0:
  10.2 19.4 all-gather.2
  32.4 49.0 all-gather.4
  89.4 128.4 all-reduce.2
  220.2 20.6 reduce-scatter.1
  244.8 78.1 all-reduce.4

commit v2 on v1

v2 whole, which is shorter than its diff:
```python
import functools

import jax
import jax.numpy as jnp
from jax import lax
from jax.experimental import pallas as pl
from jax.experimental.pallas import tpu as pltpu
from jax.sharding import PartitionSpec as P

f32, bf16 = jnp.float32, jnp.bfloat16
NN, NT = ((1,), (0,)), ((1,), (1,))


def split(x):
    high = x.astype(bf16)
    return high, (x - high.astype(f32)).astype(bf16)


def mul(a, b, dims=NN):
    def one(x, y):
        return lax.dot_general(x, y, (dims, ((), ())), preferred_element_type=f32)

    return one(a[0], b[0]) + (one(a[0], b[1]) + one(a[1], b[0]))


def start(axis, n, me, source, target, send, recv):
    copies = []
    for d in range(1, n):
        peer = lax.rem(me + d, n)
        copy = pltpu.make_async_remote_copy(
            src_ref=source(peer),
            dst_ref=target,
            send_sem=send.at[d],
            recv_sem=recv.at[d],
            device_id={axis: peer},
            device_id_type=pl.DeviceIdType.MESH,
        )
        copy.start()
        copies.append(copy)
    return copies


def arrive(copies):
    for copy in copies:
        copy.wait_recv()


def kernel(
    nr, nc, a_hbm, u_ref, l_ref, lot_ref, uol_ref, iln_ref, iun_ref, ilo_ref, iuo_ref,
    strip_ref, band_ref, small_ref,
    a_ref, ah, al, xu, xl, ut, lt, pb, ps, rb, rp, bc, part, r1, s2, r2, ag, uni, lni,
    asem, rs_send, rs_recv, cs_send, cs_recv,
):
    r, c = lax.axis_index("row"), lax.axis_index("col")
    rows, cols = a_hbm.shape
    wu, wl = cols // nr, rows // nc
    width = iln_ref.shape[0]
    hu, hl = width // nr, width // nc
    load = pltpu.make_async_copy(a_hbm, a_ref, asem)
    load.start()
    barrier = pltpu.get_barrier_semaphore()
    for d in range(1, nr):
        pl.semaphore_signal(barrier, inc=1, device_id={"row": lax.rem(r + d, nr)}, device_id_type=pl.DeviceIdType.MESH)
    for d in range(1, nc):
        pl.semaphore_signal(barrier, inc=1, device_id={"col": lax.rem(c + d, nc)}, device_id_type=pl.DeviceIdType.MESH)
    pl.semaphore_wait(barrier, nr + nc - 2)

    def ucol(i):
        return pl.ds(pl.multiple_of(i * wu, wu), wu)

    def lcol(i):
        return pl.ds(pl.multiple_of(i * wl, wl), wl)

    def row_stage(k, source, target):
        return start("row", nr, r, source, target, rs_send.at[k], rs_recv.at[k])

    def col_stage(k, source, target):
        return start("col", nc, c, source, target, cs_send.at[k], cs_recv.at[k])

    every = []
    u0 = row_stage(0, lambda p: u_ref.at[:, ucol(p)], xu.at[r])
    l0 = col_stage(0, lambda p: l_ref.at[:, lcol(p)], xl.at[c])
    xu[r] = u_ref[:, ucol(r)]
    xl[c] = l_ref[:, lcol(c)]
    iun, iuo = split(iun_ref[...]), split(iuo_ref[...])
    mix_u = split(mul(split(mul(iuo, split(uol_ref[...]))), iun))
    ilo = ilo_ref[...]
    mix_l = mul(split(mul(split(iln_ref[...]), split(lot_ref[...]))), split(ilo))
    mix_l, ilo, iln = split(mix_l.T), split(ilo.T), split(iln_ref[...].T)
    arrive(u0)
    un = split(xu[:, :hu].reshape(width, wu))
    ut[:, ucol(r)] = mul(iuo, split(xu[:, hu:].reshape(width, wu))) - mul(mix_u, un)
    u1 = row_stage(1, lambda p: ut.at[:, ucol(r)], ut.at[:, ucol(r)])
    arrive(l0)
    ln = split(xl[:, :hl].reshape(width, wl))
    lt[:, lcol(c)] = mul(ilo, split(xl[:, hl:].reshape(width, wl))) - mul(mix_l, ln)
    l1 = col_stage(1, lambda p: lt.at[:, lcol(c)], lt.at[:, lcol(c)])
    uni[...] = mul(iun, un)
    lni[...] = mul(iln, ln)
    load.wait()
    high, low = split(a_ref[...])
    ah[...] = high
    al[...] = low
    arrive(l1)
    lts = split(lt[...])
    tile = 2 * wu
    for i in range(cols // tile):
        here = slice(i * tile, (i + 1) * tile)
        pb[:, here] = -mul(lts, (ah[:, here], al[:, here]))
    b0 = row_stage(2, lambda p: pb.at[:, ucol(p)], rb.at[r])
    rb[r] = pb[:, ucol(r)]
    arrive(u1)
    uts = split(ut[...])
    tile = 2 * wl
    for i in range(rows // tile):
        here = slice(i * tile, (i + 1) * tile)
        ps[here] = -mul((ah[here], al[here]), uts, NT)
    p0 = col_stage(2, lambda p: ps.at[lcol(p)], rp.at[c])
    rp[c] = ps[lcol(c)]
    arrive(b0)
    band = rb[0]
    for i in range(1, nr):
        band = band + rb[i]
    bc[...] = band
    arrive(p0)
    strip = rp[0]
    for i in range(1, nc):
        strip = strip + rp[i]
    strip_ref[...] = strip
    b1 = row_stage(3, lambda p: bc, band_ref.at[:, ucol(r)])
    band_ref[:, ucol(r)] = band
    part[:width] = -mul(split(band), split(uni[...]), NT)
    strip = split(strip)
    part[width : 2 * width] = -mul(split(lni[...]), strip)
    part[2 * width :] = -mul(split(lt[:, lcol(c)]), strip)
    high = 3 * width // nc
    each = high // nr
    s0 = col_stage(3, lambda p: part.at[pl.ds(pl.multiple_of(p * high, high), high)], r1.at[c])
    r1[c] = part[pl.ds(pl.multiple_of(c * high, high), high)]
    arrive(s0)
    total = r1[0]
    for i in range(1, nc):
        total = total + r1[i]
    for i in range(nr):
        s2[i] = total[i * each : (i + 1) * each]
    s1 = row_stage(4, lambda p: s2.at[p], r2.at[r])
    r2[r] = s2[r]
    arrive(s1)
    total = r2[0]
    for i in range(1, nr):
        total = total + r2[i]
    ag[r] = total
    s3 = row_stage(5, lambda p: ag.at[r], ag.at[r])
    arrive(s3)
    s4 = col_stage(4, lambda p: ag, small_ref.at[c])
    small_ref[c] = ag[...]
    arrive(s4)
    arrive(b1)
    for group in (u0, l0, u1, l1, b0, p0, b1, s0, s1, s3, s4):
        for copy in group:
            copy.wait_send()


def body(an, ln, un, lot, lo, uol, uo, dln, dun, iln, iun, dlo, duo, ilo, iuo):
    nr, nc = lax.axis_size("row"), lax.axis_size("col")
    rows, cols = an.shape
    width = iln.shape[0]
    wu, wl = cols // nr, rows // nc
    u = jnp.concatenate((un, uo), axis=0)
    l = jnp.concatenate((ln, lo), axis=1).T
    high = 3 * width // nc
    each = high // nr
    vm = pl.BlockSpec(memory_space=pltpu.VMEM)
    V = pltpu.VMEM
    strip, band, small = pl.pallas_call(
        functools.partial(kernel, nr, nc),
        out_shape=(
            jax.ShapeDtypeStruct((wl, width), f32),
            jax.ShapeDtypeStruct((width, cols), f32),
            jax.ShapeDtypeStruct((nc, nr, each, width), f32),
        ),
        in_specs=[pl.BlockSpec(memory_space=pl.ANY)] + [vm] * 8,
        out_specs=(vm, vm, vm),
        scratch_shapes=[
            V((rows, cols), f32), V((rows, cols), bf16), V((rows, cols), bf16),
            V((nr, 2 * width // nr, wu), f32), V((nc, 2 * width // nc, wl), f32),
            V((width, cols), f32), V((width, rows), f32),
            V((width, cols), f32), V((rows, width), f32),
            V((nr, width, wu), f32), V((nc, wl, width), f32),
            V((width, wu), f32), V((3 * width, width), f32),
            V((nc, high, width), f32), V((nr, each, width), f32),
            V((nr, each, width), f32), V((nr, each, width), f32),
            V((width, wu), f32), V((width, wl), f32),
            pltpu.SemaphoreType.DMA,
            pltpu.SemaphoreType.DMA((6, nr)), pltpu.SemaphoreType.DMA((6, nr)),
            pltpu.SemaphoreType.DMA((5, nc)), pltpu.SemaphoreType.DMA((5, nc)),
        ],
        compiler_params=pltpu.CompilerParams(collective_id=0, has_side_effects=True),
    )(an, u, l, lot, uol, iln, iun, ilo, iuo)
    small = small.reshape(3 * width, width)
    return small[2 * width :], small[width : 2 * width], strip, small[:width], band


def solution(mesh):
    two, whole = P("row", "col"), P()
    return jax.shard_map(
        body,
        mesh=mesh,
        in_specs=(two, two, two, whole, two, whole, two) + (whole,) * 8,
        out_specs=(P(), P(), P(("row", "col"), None), P(), P(None, "col")),
        check_vma=False,
    )
```

time: 332 us -> 119 us (0.36)
  waiting for transfers between devices: 288 us -> 0 us
  Pallas kernels: 0 us -> 109 us
  matrix products: 15.8 us -> 0 us
  between operations: 14 us -> 0.65 us
  local copies, waits for them, and re-layouts: 9.28 us -> 4.63 us
    psum x2 -> x0, waiting for transfers between devices: 208 us -> none  [the longest x1 127 us: body(): small = lax.psum(jnp.concatenate((left, both), axis=0), ('row', 'col'))]
    pallas_call x0 -> x1, Pallas kernels: none -> 109 us  [body(): pl.pallas_call(functools.partial(kernel, nr, nc), out_shape=(jax.ShapeDty...]
    all_gather x2 -> x0, waiting for transfers between devices: 61.9 us -> none  [the longest x1 46.1 us: body(): lax.all_gather(jnp.concatenate((un[None], uo[None])), 'row', axis=1, tile...]
    reduce_scatter x1 -> x0, waiting for transfers between devices: 17.2 us -> none  [body(): strip = lax.psum_scatter(strip, 'col', scatter_dimension=0, tiled=True)]
    dot_general x14 -> x0, matrix products: 15.8 us -> none  [dot(): lax.dot_general(left, right, (((a,), (b,)), ((), ())), precision=precise)]
  transfers between devices with their start and end apart: 5 -> 0, of which waited for: 5 -> 0; matrix products, arithmetic and copies ran while one was open for 5% -> 0% of each run, Pallas kernels for 0% -> 0%
where the time goes in v2:
time: 119 us; the launch traced here: 117 us
  Pallas kernels  109 us (92%)
  local copies, waits for them, and re-layouts  4.63 us (4%)
  other arithmetic  3.38 us (3%)
    pallas_call x1, Pallas kernels, body(): pl.pallas_call(functools.partial(kernel, nr, nc), out_shape=(jax.ShapeDty...  109 us
    unnamed x4, local copies, waits for them, and re-layouts  2.54 us

profile of v2, /device:TPU:0, one launch (start us, length us, event | category | flops | bytes accessed | tf_op | source)
XLA Modules:
  0.0 117.4 jit_solution(15265238132849112976)
XLA Ops:
  0.6 1.7 %maximum_bitcast_fusion.l_ref = f32[128,512]{1,0:T(8,128)} fusion(f32[512,64]{0,1:T(8,128)} %param.19, f32[512,64]{0,1:T(8,128)} %param.16), kind=kLoop, calls=%fused_computation.1 | loop fusion | flops 65536 | bytes 524288 | tf_op jit(solution)/shard_map/transpose | solution.py:170
  2.3 1.7 %pad_maximum_fusion.u_ref = f32[64,1024]{1,0:T(8,128)} fusion(f32[32,1024]{1,0:T(8,128)} %param.21, f32[32,1024]{1,0:T(8,128)} %param.17), kind=kLoop, calls=%fused_computation | loop fusion | flops 65536 | bytes 524288 | tf_op jit(solution)/shard_map/concatenate | solution.py:169
  4.0 108.7 %shard_map.146 = (f32[128,256]{1,0:T(8,128)}, f32[256,1024]{1,0:T(8,128)}, f32[4,8,24,256]{3,2,1,0:T(8,128)}) custom-call(f32[512,1024]{1,0:T(8,128)} %a_hbm.1, f32[64,1024]{1,0:T(8,128)} %pad_maximum_fusion.u_ref, f32[128,512]{1,0:T(8,128)} %maximum_bitcast_fusion.l_ref, f32[256,256]{1,0:T(8,128)} %lot_ref.1, f32[256,256]{1,0:T(8,128)} %uol_ref.1, ...), custom_call_target="tpu_custom_call" | custom-call | tf_op jit(solution)/shard_map/pallas_call | solution.py:175
  112.7 0.0 copy-start
  112.7 2.1 %fusion = (f32[256,256]{1,0:T(8,128)}, f32[256,256]{1,0:T(8,128)}, f32[256,256]{1,0:T(8,128)}) fusion(f32[768,256]{1,0:T(8,128)} %bitcast.3), kind=kLoop, calls=%fused_computation.2 | loop fusion | bytes 1572864 | tf_op jit(solution)/shard_map/slice | solution.py:201
  114.8 1.6 %copy.18 = f32[128,256]{1,0:T(8,128)} copy(f32[128,256]{1,0:T(8,128)} %get-tuple-element.21) | data formatting | bytes 262144
  116.4 0.0 copy-done
  116.4 1.0 copy.19
Async XLA Ops:
  112.7 3.7 %copy-start = (f32[256,1024]{1,0:T(8,128)S(1)}, f32[256,1024]{1,0:T(8,128)}, u32[]{:S(2)}) copy-start(f32[256,1024]{1,0:T(8,128)} %get-tuple-element.23) | copy-start | bytes 3145732

commit v3 on v2

v3 whole, which is shorter than its diff:
```python
import functools

import jax
import jax.numpy as jnp
from jax import lax
from jax.experimental import pallas as pl
from jax.experimental.pallas import tpu as pltpu
from jax.sharding import PartitionSpec as P

f32, bf16 = jnp.float32, jnp.bfloat16
NN, NT = ((1,), (0,)), ((1,), (1,))


def split(x):
    high = x.astype(bf16)
    return high, (x - high.astype(f32)).astype(bf16)


def mul(a, b, dims=NN):
    def one(x, y):
        return lax.dot_general(x, y, (dims, ((), ())), preferred_element_type=f32)

    return one(a[0], b[0]) + (one(a[0], b[1]) + one(a[1], b[0]))


def start(axis, n, me, source, target, send, recv):
    copies = []
    for d in range(1, n):
        peer = lax.rem(me + d, n)
        copy = pltpu.make_async_remote_copy(
            src_ref=source(peer),
            dst_ref=target,
            send_sem=send.at[d],
            recv_sem=recv.at[d],
            device_id={axis: peer},
            device_id_type=pl.DeviceIdType.MESH,
        )
        copy.start()
        copies.append(copy)
    return copies


def arrive(copies):
    for copy in copies:
        copy.wait_recv()


def kernel(
    nr, nc, ny, a_hbm, u_ref, l_ref, lot_ref, uol_ref, iln_ref, iun_ref, ilo_ref, iuo_ref,
    strip_ref, band_ref, both_ref, left_ref,
    a_ref, ah, al, xu, xl, ut, lt, pb, ps, ry, sz, rz, rp, bc, uni, lni,
    pa, ra, sa, ta, ga, pl_, rl, sl, tl, gl,
    asem, rs_send, rs_recv, cs_send, cs_recv,
):
    r, c = lax.axis_index("row"), lax.axis_index("col")
    rows, cols = a_hbm.shape
    wu, wl = cols // nr, rows // nc
    width = iln_ref.shape[0]
    hu, hl = width // nr, width // nc
    nz = nr // ny
    z, y = r // ny, lax.rem(r, ny)
    far = [nz // 2] * (nz > 1) + [k for k in range(nz - 1, 0, -1) if k != nz // 2]
    load = pltpu.make_async_copy(a_hbm, a_ref, asem)
    load.start()
    barrier = pltpu.get_barrier_semaphore()
    for d in range(1, nr):
        pl.semaphore_signal(barrier, inc=1, device_id={"row": lax.rem(r + d, nr)}, device_id_type=pl.DeviceIdType.MESH)
    for d in range(1, nc):
        pl.semaphore_signal(barrier, inc=1, device_id={"col": lax.rem(c + d, nc)}, device_id_type=pl.DeviceIdType.MESH)
    pl.semaphore_wait(barrier, nr + nc - 2)

    def ucol(i):
        return pl.ds(pl.multiple_of(i * wu, wu), wu)

    def lcol(i):
        return pl.ds(pl.multiple_of(i * wl, wl), wl)

    sent = []

    def row_stage(k, source, target):
        copies = start("row", nr, r, source, target, rs_send.at[k], rs_recv.at[k])
        sent.extend(copies)
        return copies

    def col_stage(k, source, target):
        copies = start("col", nc, c, source, target, cs_send.at[k], cs_recv.at[k])
        sent.extend(copies)
        return copies

    def push(stage, index, source, target, zi, yi):
        copy = pltpu.make_async_remote_copy(
            src_ref=source,
            dst_ref=target,
            send_sem=rs_send.at[stage, index],
            recv_sem=rs_recv.at[stage, index],
            device_id={"row": zi * ny + yi},
            device_id_type=pl.DeviceIdType.MESH,
        )
        copy.start()
        sent.append(copy)
        return copy

    def across(stage, k, source, slot):
        return [push(stage, k * ny + d, source, slot, z, lax.rem(y + d, ny)) for d in range(1, ny)]

    def gather_start(stage, source, slot):
        along = {k: push(stage, k, source, slot(r), lax.rem(z + k, nz), y) for k in far}
        return along, across(stage + 1, 0, source, slot(r))

    def gather_pass(stage, state, slot):
        along, over = state
        for k in far[::-1]:
            along[k].wait_recv()
            here = slot(lax.rem(z - k + nz, nz) * ny + y)
            over.extend(across(stage + 1, k, here, here))
        return over

    u0 = row_stage(0, lambda p: u_ref.at[:, ucol(p)], xu.at[r])
    l0 = col_stage(0, lambda p: l_ref.at[:, lcol(p)], xl.at[c])
    xu[r] = u_ref[:, ucol(r)]
    xl[c] = l_ref[:, lcol(c)]
    iun, iuo = split(iun_ref[...]), split(iuo_ref[...])
    mix_u = split(mul(split(mul(iuo, split(uol_ref[...]))), iun))
    ilo = ilo_ref[...]
    mix_l = mul(split(mul(split(iln_ref[...]), split(lot_ref[...]))), split(ilo))
    mix_l, ilo, iln = split(mix_l.T), split(ilo.T), split(iln_ref[...].T)
    arrive(u0)
    un = split(xu[:, :hu].reshape(width, wu))
    ut[:, ucol(r)] = mul(iuo, split(xu[:, hu:].reshape(width, wu))) - mul(mix_u, un)
    uslot = lambda i: ut.at[:, ucol(i)]
    u1 = gather_start(1, uslot(r), uslot)
    arrive(l0)
    ln = split(xl[:, :hl].reshape(width, wl))
    lt[:, lcol(c)] = mul(ilo, split(xl[:, hl:].reshape(width, wl))) - mul(mix_l, ln)
    l1 = col_stage(1, lambda p: lt.at[:, lcol(c)], lt.at[:, lcol(c)])
    uni[...] = mul(iun, un)
    lni[...] = mul(iln, ln)
    load.wait()
    high, low = split(a_ref[...])
    ah[...] = high
    al[...] = low
    arrive(l1)
    lts = split(lt[...])
    tile = 2 * wu
    for i in range(cols // tile):
        here = slice(i * tile, (i + 1) * tile)
        pb[:, here] = -mul(lts, (ah[:, here], al[:, here]))
    b0 = {}
    for k in far + [0]:
        zt = lax.rem(z + k, nz)
        b0[k] = [
            push(3, k * ny + d, pb.at[:, ucol(zt * ny + lax.rem(y + d, ny))], ry.at[k, d], z, lax.rem(y + d, ny))
            for d in range(1, ny)
        ]
    over = gather_pass(1, u1, uslot)
    b1 = {}
    for k in far + [0]:
        arrive(b0[k])
        zt = lax.rem(z + k, nz)
        total = pb[:, ucol(zt * ny + y)]
        for d in range(1, ny):
            total = total + ry[k, d]
        if k:
            sz[k] = total
            b1[k] = push(4, k, sz.at[k], rz.at[k], zt, y)
        else:
            rz[0] = total
    arrive(over)
    uts = split(ut[...])
    tile = 2 * wl
    for i in range(rows // tile):
        here = slice(i * tile, (i + 1) * tile)
        ps[here] = -mul((ah[here], al[here]), uts, NT)
    p0 = col_stage(2, lambda p: ps.at[lcol(p)], rp.at[c])
    rp[c] = ps[lcol(c)]

    def small_cols(stage, part, got):
        high = part.shape[0] // nc
        at = lambda p: part.at[pl.ds(pl.multiple_of(p * high, high), high)]
        copies = col_stage(stage, at, got.at[c])
        got[c] = part[pl.ds(pl.multiple_of(c * high, high), high)]
        return copies

    def small_rows(stage, copies, got, send, take):
        arrive(copies)
        total = got[0]
        for i in range(1, nc):
            total = total + got[i]
        each = send.shape[1]
        for i in range(nr):
            send[i] = total[i * each : (i + 1) * each]
        copies = row_stage(stage, lambda p: send.at[p], take.at[r])
        take[r] = send[r]
        return copies

    def back_rows(stage, copies, take, whole):
        arrive(copies)
        total = take[0]
        for i in range(1, nr):
            total = total + take[i]
        whole[r] = total
        return row_stage(stage, lambda p: whole.at[r], whole.at[r])

    def back_cols(stage, copies, whole, out):
        arrive(copies)
        copies = col_stage(stage, lambda p: whole, out.at[c])
        out[c] = whole[...]
        return copies

    arrive([b1[k] for k in far])
    band = rz[0]
    for k in range(1, nz):
        band = band + rz[k]
    bc[...] = band
    bslot = lambda i: band_ref.at[:, ucol(i)]
    b2 = gather_start(5, bc, bslot)
    band_ref[:, ucol(r)] = band
    pl_[...] = -mul(split(band), split(uni[...]), NT)
    left = small_cols(3, pl_, rl)
    arrive(p0)
    strip = rp[0]
    for i in range(1, nc):
        strip = strip + rp[i]
    strip_ref[...] = strip
    strip = split(strip)
    pa[:width] = -mul(split(lni[...]), strip)
    pa[width:] = -mul(split(lt[:, lcol(c)]), strip)
    both = small_cols(4, pa, ra)
    left = small_rows(7, left, rl, sl, tl)
    both = small_rows(8, both, ra, sa, ta)
    left = back_rows(9, left, tl, gl)
    both = back_rows(10, both, ta, ga)
    left = back_cols(5, left, gl, left_ref)
    both = back_cols(6, both, ga, both_ref)
    over = gather_pass(5, b2, bslot)
    arrive(left)
    arrive(both)
    arrive(over)
    for copy in sent:
        copy.wait_send()


def body(an, ln, un, lot, lo, uol, uo, dln, dun, iln, iun, dlo, duo, ilo, iuo):
    nr, nc = lax.axis_size("row"), lax.axis_size("col")
    rows, cols = an.shape
    width = iln.shape[0]
    wu, wl = cols // nr, rows // nc
    u = jnp.concatenate((un, uo), axis=0)
    l = jnp.concatenate((ln, lo), axis=1).T
    ny = nc // 2 if nc % 2 == 0 and nr % max(nc // 2, 1) == 0 else 1
    nz = nr // ny
    vm = pl.BlockSpec(memory_space=pltpu.VMEM)
    V = pltpu.VMEM

    def chain(size):
        high = size // nc
        whole = V((nr, high // nr, width), f32)
        return [V((size, width), f32), V((nc, high, width), f32), whole, whole, whole]

    D = pltpu.SemaphoreType.DMA
    strip, band, both, left = pl.pallas_call(
        functools.partial(kernel, nr, nc, ny),
        out_shape=(
            jax.ShapeDtypeStruct((wl, width), f32),
            jax.ShapeDtypeStruct((width, cols), f32),
            jax.ShapeDtypeStruct((nc, nr, 2 * width // nc // nr, width), f32),
            jax.ShapeDtypeStruct((nc, nr, width // nc // nr, width), f32),
        ),
        in_specs=[pl.BlockSpec(memory_space=pl.ANY)] + [vm] * 8,
        out_specs=(vm, vm, vm, vm),
        scratch_shapes=[
            V((rows, cols), f32), V((rows, cols), bf16), V((rows, cols), bf16),
            V((nr, 2 * width // nr, wu), f32), V((nc, 2 * width // nc, wl), f32),
            V((width, cols), f32), V((width, rows), f32),
            V((width, cols), f32), V((rows, width), f32),
            V((nz, ny, width, wu), f32), V((nz, width, wu), f32), V((nz, width, wu), f32),
            V((nc, wl, width), f32), V((width, wu), f32),
            V((width, wu), f32), V((width, wl), f32),
            *chain(2 * width), *chain(width),
            D, D((11, nr)), D((11, nr)), D((7, nc)), D((7, nc)),
        ],
        compiler_params=pltpu.CompilerParams(collective_id=0, has_side_effects=True),
    )(an, u, l, lot, uol, iln, iun, ilo, iuo)
    both = both.reshape(2 * width, width)
    return both[width:], both[:width], strip, left.reshape(width, width), band


def solution(mesh):
    two, whole = P("row", "col"), P()
    return jax.shard_map(
        body,
        mesh=mesh,
        in_specs=(two, two, two, whole, two, whole, two) + (whole,) * 8,
        out_specs=(P(), P(), P(("row", "col"), None), P(), P(None, "col")),
        check_vma=False,
    )
```

time: 119 us -> 94.7 us (0.80); the launches traced: 117 us -> 94.5 us
  Pallas kernels: 109 us -> 84.3 us
  local copies, waits for them, and re-layouts: 4.63 us -> 6.15 us
    pallas_call x1, Pallas kernels: 109 us -> 84.3 us  [body(): pl.pallas_call(functools.partial(kernel, nr, nc, ny), out_shape=(jax.Shap...]
    unnamed x4 -> x5, local copies, waits for them, and re-layouts: 2.54 us -> 4.21 us
where the time goes in v3:
time: 94.7 us; the launch traced here: 94.5 us
  Pallas kernels  84.3 us (89%)
  local copies, waits for them, and re-layouts  6.15 us (6%)
  other arithmetic  3.38 us (4%)
    pallas_call x1, Pallas kernels, body(): pl.pallas_call(functools.partial(kernel, nr, nc, ny), out_shape=(jax.Shap...  84.3 us
    unnamed x5, local copies, waits for them, and re-layouts  4.21 us
    slice x1, local copies, waits for them, and re-layouts, body(): return (both[width:], both[:width], strip, left.reshape(width, width), band)  1.94 us

profile of v3, /device:TPU:0, one launch (start us, length us, event | category | flops | bytes accessed | tf_op | source)
XLA Modules:
  0.0 94.5 jit_solution(13848355719765594207)
XLA Ops:
  0.6 1.7 %maximum_bitcast_fusion.l_ref = f32[128,512]{1,0:T(8,128)} fusion(f32[512,64]{0,1:T(8,128)} %param.19, f32[512,64]{0,1:T(8,128)} %param.16), kind=kLoop, calls=%fused_computation.1 | loop fusion | flops 65536 | bytes 524288 | tf_op jit(solution)/shard_map/transpose | solution.py:249
  2.3 1.7 %pad_maximum_fusion.u_ref = f32[64,1024]{1,0:T(8,128)} fusion(f32[32,1024]{1,0:T(8,128)} %param.21, f32[32,1024]{1,0:T(8,128)} %param.17), kind=kLoop, calls=%fused_computation | loop fusion | flops 65536 | bytes 524288 | tf_op jit(solution)/shard_map/concatenate | solution.py:248
  4.0 84.3 %shard_map.146 = (f32[128,256]{1,0:T(8,128)}, f32[256,1024]{1,0:T(8,128)}, f32[4,8,16,256]{3,2,1,0:T(8,128)}, f32[4,8,8,256]{3,2,1,0:T(8,128)}) custom-call(f32[512,1024]{1,0:T(8,128)} %a_hbm.1, f32[64,1024]{1,0:T(8,128)} %pad_maximum_fusion.u_ref, f32[128,512]{1,0:T(8,128)} %maximum_bitcast_fusion.l_ref, f32[256,256]{1,0:T(8,128)} %lot_ref.1, ...), custom_call_target="tpu_custom_call" | custom-call | tf_op jit(solution)/shard_map/pallas_call | solution.py:261
  88.3 0.0 copy-start
  88.3 1.9 %fusion = (f32[2,8,16,256]{3,2,1,0:T(8,128)}, f32[2,8,16,256]{3,2,1,0:T(8,128)}) fusion(f32[4,8,16,256]{3,2,1,0:T(8,128)} %get-tuple-element.9), kind=kLoop, calls=%fused_computation.2 | loop fusion | bytes 1048576 | tf_op jit(solution)/shard_map/slice | solution.py:285
  90.2 1.6 %copy.19 = f32[128,256]{1,0:T(8,128)} copy(f32[128,256]{1,0:T(8,128)} %get-tuple-element.22) | data formatting | bytes 262144
  91.8 1.7 %copy.20 = f32[256,256]{1,0:T(8,128)} copy(f32[256,256]{1,0:T(8,128)} %bitcast.5) | data formatting | bytes 524288
  93.5 0.0 copy-done
  93.5 1.0 %copy.21 = f32[256,1024]{1,0:T(8,128)} copy(f32[256,1024]{1,0:T(8,128)S(1)} %copy-done) | data formatting | bytes 2097152
Async XLA Ops:
  88.3 5.2 %copy-start = (f32[256,1024]{1,0:T(8,128)S(1)}, f32[256,1024]{1,0:T(8,128)}, u32[]{:S(2)}) copy-start(f32[256,1024]{1,0:T(8,128)} %get-tuple-element.24) | copy-start | bytes 3145732

commit v4 on v3

--- a/solution.py
+++ b/solution.py
@@ -46,21 +46,25 @@
 
 
 def kernel(
-    nr, nc, ny, a_hbm, u_ref, l_ref, lot_ref, uol_ref, iln_ref, iun_ref, ilo_ref, iuo_ref,
+    nr, nc, ny, a_hbm, un_ref, uo_ref, l_ref, lot_hbm, uol_hbm, iln_hbm, iun_hbm, ilo_hbm, iuo_hbm,
     strip_ref, band_ref, both_ref, left_ref,
     a_ref, ah, al, xu, xl, ut, lt, pb, ps, ry, sz, rz, rp, bc, uni, lni,
     pa, ra, sa, ta, ga, pl_, rl, sl, tl, gl,
-    asem, rs_send, rs_recv, cs_send, cs_recv,
+    sq, asem, qsem, rs_send, rs_recv, cs_send, cs_recv,
 ):
     r, c = lax.axis_index("row"), lax.axis_index("col")
     rows, cols = a_hbm.shape
     wu, wl = cols // nr, rows // nc
-    width = iln_ref.shape[0]
-    hu, hl = width // nr, width // nc
+    width = iln_hbm.shape[0]
+    hl = width // nc
     nz = nr // ny
     z, y = r // ny, lax.rem(r, ny)
     far = [nz // 2] * (nz > 1) + [k for k in range(nz - 1, 0, -1) if k != nz // 2]
     load = pltpu.make_async_copy(a_hbm, a_ref, asem)
+    squares = (iuo_hbm, uol_hbm, iun_hbm, iln_hbm, lot_hbm, ilo_hbm)
+    loads = [pltpu.make_async_copy(m, sq.at[i], qsem.at[i]) for i, m in enumerate(squares)]
+    for copy in loads:
+        copy.start()
     load.start()
     barrier = pltpu.get_barrier_semaphore()
     for d in range(1, nr):
@@ -115,18 +119,22 @@
             over.extend(across(stage + 1, k, here, here))
         return over
 
-    u0 = row_stage(0, lambda p: u_ref.at[:, ucol(p)], xu.at[r])
+    u0 = row_stage(0, lambda p: un_ref.at[:, ucol(p)], xu.at[0, r])
+    u0 = u0 + row_stage(11, lambda p: uo_ref.at[:, ucol(p)], xu.at[1, r])
     l0 = col_stage(0, lambda p: l_ref.at[:, lcol(p)], xl.at[c])
-    xu[r] = u_ref[:, ucol(r)]
+    xu[0, r] = un_ref[:, ucol(r)]
+    xu[1, r] = uo_ref[:, ucol(r)]
     xl[c] = l_ref[:, lcol(c)]
-    iun, iuo = split(iun_ref[...]), split(iuo_ref[...])
-    mix_u = split(mul(split(mul(iuo, split(uol_ref[...]))), iun))
-    ilo = ilo_ref[...]
-    mix_l = mul(split(mul(split(iln_ref[...]), split(lot_ref[...]))), split(ilo))
-    mix_l, ilo, iln = split(mix_l.T), split(ilo.T), split(iln_ref[...].T)
+    for copy in loads:
+        copy.wait()
+    iuo, iun = split(sq[0]), split(sq[2])
+    mix_u = split(mul(split(mul(iuo, split(sq[1]))), iun))
+    ilo = sq[5]
+    mix_l = mul(split(mul(split(sq[3]), split(sq[4]))), split(ilo))
+    mix_l, ilo, iln = split(mix_l.T), split(ilo.T), split(sq[3].T)
     arrive(u0)
-    un = split(xu[:, :hu].reshape(width, wu))
-    ut[:, ucol(r)] = mul(iuo, split(xu[:, hu:].reshape(width, wu))) - mul(mix_u, un)
+    un = split(xu[0].reshape(width, wu))
+    ut[:, ucol(r)] = mul(iuo, split(xu[1].reshape(width, wu))) - mul(mix_u, un)
     uslot = lambda i: ut.at[:, ucol(i)]
     u1 = gather_start(1, uslot(r), uslot)
     arrive(l0)
@@ -228,11 +236,11 @@
     both = small_cols(4, pa, ra)
     left = small_rows(7, left, rl, sl, tl)
     both = small_rows(8, both, ra, sa, ta)
+    over = gather_pass(5, b2, bslot)
     left = back_rows(9, left, tl, gl)
     both = back_rows(10, both, ta, ga)
     left = back_cols(5, left, gl, left_ref)
     both = back_cols(6, both, ga, both_ref)
-    over = gather_pass(5, b2, bslot)
     arrive(left)
     arrive(both)
     arrive(over)
@@ -245,11 +253,11 @@
     rows, cols = an.shape
     width = iln.shape[0]
     wu, wl = cols // nr, rows // nc
-    u = jnp.concatenate((un, uo), axis=0)
     l = jnp.concatenate((ln, lo), axis=1).T
     ny = nc // 2 if nc % 2 == 0 and nr % max(nc // 2, 1) == 0 else 1
     nz = nr // ny
     vm = pl.BlockSpec(memory_space=pltpu.VMEM)
+    hbm = pl.BlockSpec(memory_space=pl.ANY)
     V = pltpu.VMEM
 
     def chain(size):
@@ -266,21 +274,21 @@
             jax.ShapeDtypeStruct((nc, nr, 2 * width // nc // nr, width), f32),
             jax.ShapeDtypeStruct((nc, nr, width // nc // nr, width), f32),
         ),
-        in_specs=[pl.BlockSpec(memory_space=pl.ANY)] + [vm] * 8,
+        in_specs=[hbm, vm, vm, vm] + [hbm] * 6,
         out_specs=(vm, vm, vm, vm),
         scratch_shapes=[
             V((rows, cols), f32), V((rows, cols), bf16), V((rows, cols), bf16),
-            V((nr, 2 * width // nr, wu), f32), V((nc, 2 * width // nc, wl), f32),
+            V((2, nr, width // nr, wu), f32), V((nc, 2 * width // nc, wl), f32),
             V((width, cols), f32), V((width, rows), f32),
             V((width, cols), f32), V((rows, width), f32),
             V((nz, ny, width, wu), f32), V((nz, width, wu), f32), V((nz, width, wu), f32),
             V((nc, wl, width), f32), V((width, wu), f32),
             V((width, wu), f32), V((width, wl), f32),
             *chain(2 * width), *chain(width),
-            D, D((11, nr)), D((11, nr)), D((7, nc)), D((7, nc)),
+            V((6, width, width), f32), D, D((6,)), D((12, nr)), D((12, nr)), D((7, nc)), D((7, nc)),
         ],
         compiler_params=pltpu.CompilerParams(collective_id=0, has_side_effects=True),
-    )(an, u, l, lot, uol, iln, iun, ilo, iuo)
+    )(an, un, uo, l, lot, uol, iln, iun, ilo, iuo)
     both = both.reshape(2 * width, width)
     return both[width:], both[:width], strip, left.reshape(width, width), band
 

time: 94.7 us -> 91.8 us (0.969); the launches traced: 94.5 us -> 90.5 us
  Pallas kernels: 84.3 us -> 82 us
  other arithmetic: 3.38 us -> 1.69 us
    pallas_call x1, Pallas kernels: 84.3 us -> 82 us  [body(): pl.pallas_call(functools.partial(kernel, nr, nc, ny), out_shape=(jax.Shap...]
    concatenate x1 -> x0, other arithmetic: 1.69 us -> none  [body(): u = jnp.concatenate((un, uo), axis=0)]
where the time goes in v4:
time: 91.8 us; the launch traced here: 90.5 us
  Pallas kernels  82 us (89%)
  local copies, waits for them, and re-layouts  6.15 us (7%)
  other arithmetic  1.69 us (2%)
    pallas_call x1, Pallas kernels, body(): pl.pallas_call(functools.partial(kernel, nr, nc, ny), out_shape=(jax.Shap...  82 us
    unnamed x5, local copies, waits for them, and re-layouts  4.21 us
    slice x1, local copies, waits for them, and re-layouts, body(): return (both[width:], both[:width], strip, left.reshape(width, width), band)  1.94 us

profile of v4, /device:TPU:0, one launch (start us, length us, event | category | flops | bytes accessed | tf_op | source)
XLA Modules:
  0.0 90.5 jit_solution(17561581161933989598)
XLA Ops:
  0.6 1.7 %maximum_bitcast_fusion.l_ref = f32[128,512]{1,0:T(8,128)} fusion(f32[512,64]{0,1:T(8,128)} %param.19, f32[512,64]{0,1:T(8,128)} %param.16), kind=kLoop, calls=%fused_computation | loop fusion | flops 65536 | bytes 524288 | tf_op jit(solution)/shard_map/transpose | solution.py:256
  2.3 82.0 %shard_map.146 = (f32[128,256]{1,0:T(8,128)}, f32[256,1024]{1,0:T(8,128)}, f32[4,8,16,256]{3,2,1,0:T(8,128)}, f32[4,8,8,256]{3,2,1,0:T(8,128)}) custom-call(f32[512,1024]{1,0:T(8,128)} %a_hbm.1, f32[32,1024]{1,0:T(8,128)} %un_ref.1, f32[32,1024]{1,0:T(8,128)} %uo_ref.1, f32[128,512]{1,0:T(8,128)} %maximum_bitcast_fusion.l_ref, f32[256,256]{1,0:T(8,128)} %lot_hbm.1, ...), custom_call_target="tpu_custom_call" | custom-call | tf_op jit(solution)/shard_map/pallas_call | solution.py:269
  84.3 0.0 copy-start
  84.3 1.9 %fusion = (f32[2,8,16,256]{3,2,1,0:T(8,128)}, f32[2,8,16,256]{3,2,1,0:T(8,128)}) fusion(f32[4,8,16,256]{3,2,1,0:T(8,128)} %get-tuple-element.9), kind=kLoop, calls=%fused_computation.1 | loop fusion | bytes 1048576 | tf_op jit(solution)/shard_map/slice | solution.py:293
  86.3 1.6 %copy.19 = f32[128,256]{1,0:T(8,128)} copy(f32[128,256]{1,0:T(8,128)} %get-tuple-element.22) | data formatting | bytes 262144
  87.8 1.7 %copy.20 = f32[256,256]{1,0:T(8,128)} copy(f32[256,256]{1,0:T(8,128)} %bitcast.5) | data formatting | bytes 524288
  89.5 0.0 copy-done
  89.5 1.0 %copy.21 = f32[256,1024]{1,0:T(8,128)} copy(f32[256,1024]{1,0:T(8,128)S(1)} %copy-done) | data formatting | bytes 2097152
Async XLA Ops:
  84.3 5.2 %copy-start = (f32[256,1024]{1,0:T(8,128)S(1)}, f32[256,1024]{1,0:T(8,128)}, u32[]{:S(2)}) copy-start(f32[256,1024]{1,0:T(8,128)} %get-tuple-element.24) | copy-start | bytes 3145732
